TPU v7x, 32 devices: a whole 2x2x4 slice. The times are simulated.
32 devices in a mesh: cores: 2 (over y), gz: 4 (over z), gy: 2 (over x), col: 2 (over core).
Axes of the slice: x: 2, y: 2, z: 4, core: 2. Of those that a mesh axis runs over, the one named last changes fastest.
Arguments:
- density: bfloat16 [32, 64, 512], P(('cores', 'gz'), 'gy', 'col'), parts along dimension 0, may hold values from -6 to 6
- first_kernel: bfloat16 [27, 8, 1], replicated, may hold values from -1.25 to 1.25
- first_bias: float32 [8], replicated, may hold values from -3 to 3
- second_kernel: bfloat16 [27, 2, 8], replicated, may hold values from -0.625 to 0.625
- second_bias: float32 [2], replicated, may hold values from -3 to 3
- owners: int32 [8, 2, 2, 16, 1], P(('cores', 'gz'), 'gy', 'col'), parts along dimension 0, may hold values from 0 to 3; in each aligned block of 16 rows (0 to 15, 16 to 31, ..., all dimensions but the last counted through in order) at most 8 rows name the same one
- solutes: float32 [8, 2, 2, 32, 2, 4, 4, 128], P(('cores', 'gz'), 'gy', 'col'), parts along dimension 0, may hold values from 0.2 to 2
- biomass: bfloat16 [8, 2, 2, 32, 4, 4, 128], P(('cores', 'gz'), 'gy', 'col'), parts along dimension 0, may hold values from 0.099609375 to 1
Outputs:
- fractions: bfloat16 [2, 32, 64, 512], P(None, ('cores', 'gz'), 'gy', 'col'), parts along dimension 1
- solutes_next: float32 [8, 2, 2, 32, 2, 4, 4, 128], P(('cores', 'gz'), 'gy', 'col'), parts along dimension 0
There are 2 independent parts, one for each index of `cores`. A program takes and returns all parts, laid end to end along the dimension named above; an argument that names none is the same for every part. Nothing has to cross between parts.
Inputs may be any that keep to these rules, and one draw needn't show every extreme that they name: `owners`: among the 16 bricks of one device at most 8 name the same owner, and some device reaches 8.
All inputs are finite; a program needn't handle non-finite values.
Results may differ from a plain program's by a relative error of at most 0.0034.
Values may be sent and summed in bfloat16 or wider, within the bound.
A program may use at most 64 MiB of HBM per device.

v0:
```python
import jax
import jax.numpy as jnp
from jax import lax
from jax.sharding import PartitionSpec as P

BY = 4
BX = 128
STEPS = 4


def extended(array, sides, width):
    for axis, dim in sides:
        size, length = (lax.axis_size(axis), array.shape[dim])
        up = [(i, (i + 1) % size) for i in range(size - 1)]
        down = [(j, i) for i, j in up]
        last = lax.slice_in_dim(array, length - width, length, axis=dim)
        initial = lax.slice_in_dim(array, 0, width, axis=dim)
        before = lax.ppermute(last, axis, up)
        after = lax.ppermute(initial, axis, down)
        array = jnp.concatenate([before, array, after], axis=dim)
    return array


def conv_layer(padded, weights, depth, rows, columns):
    total = jnp.zeros((weights.shape[1], depth, rows, columns), jnp.float32)
    for offset in range(27):
        shift_z = offset // 9
        shift_y = offset // 3 % 3
        shift_x = offset % 3
        window = padded[
            :, shift_z : shift_z + depth, shift_y : shift_y + rows, shift_x : shift_x + columns
        ]
        total = total + jnp.einsum(
            "oc,czyx->ozyx", weights[offset], window, preferred_element_type=jnp.float32
        )
    return total


def single_channel_conv(padded, weights, depth, rows, columns):
    windows = []
    for offset in range(27):
        shift_z = offset // 9
        shift_y = offset // 3 % 3
        shift_x = offset % 3
        windows.append(
            padded[shift_z : shift_z + depth, shift_y : shift_y + rows, shift_x : shift_x + columns]
        )
    stacked = jnp.stack(windows, axis=0)
    return jnp.einsum(
        "ko,kzyx->ozyx", weights[:, :, 0], stacked, preferred_element_type=jnp.float32
    )


def laplace(field):
    padded = jnp.pad(field, [(0, 0)] * (field.ndim - 3) + [(1, 1), (1, 1), (1, 1)], mode="edge")
    centre = padded[..., 1:-1, 1:-1, 1:-1]
    beside_all = padded[..., 2:, 1:-1, 1:-1] + padded[..., :-2, 1:-1, 1:-1]
    beside_all = beside_all + padded[..., 1:-1, 2:, 1:-1] + padded[..., 1:-1, :-2, 1:-1]
    beside_all = beside_all + padded[..., 1:-1, 1:-1, 2:] + padded[..., 1:-1, 1:-1, :-2]
    return beside_all - 6.0 * centre


def advance(state, arrived, biomass):
    pore = arrived[..., 0, :, :, :].astype(jnp.float32)
    organic = arrived[..., 1, :, :, :].astype(jnp.float32)
    mass = biomass.astype(jnp.float32)
    carbon = state[..., 0, :, :, :]
    oxygen = state[..., 1, :, :, :]
    for step in range(STEPS):
        uptake = 0.25 * mass * carbon / (0.5 + jnp.abs(carbon)) * oxygen / (0.3 + jnp.abs(oxygen))
        carbon_new = carbon + 0.12 * pore * laplace(carbon) + 0.3 * organic - uptake
        oxygen_new = oxygen + 0.16 * pore * laplace(oxygen) - uptake
        carbon, oxygen = (carbon_new, oxygen_new)
    return jnp.stack([carbon, oxygen], axis=-4)


def per_device(
    density, first_kernel, first_bias, second_kernel, second_bias, owners, solutes, biomass
):
    depth, rows, columns = density.shape
    padded = extended(density, (("gz", 0), ("gy", 1), ("col", 2)), 1)
    first = single_channel_conv(padded, first_kernel, depth, rows, columns)
    hidden = jnp.maximum(first + first_bias[:, None, None, None], 0.0).astype(jnp.bfloat16)
    hidden_pad = extended(hidden, (("gz", 1), ("gy", 2), ("col", 3)), 1)
    second = conv_layer(hidden_pad, second_kernel, depth, rows, columns)
    fractions = jax.nn.sigmoid(second + second_bias[:, None, None, None]).astype(jnp.bfloat16)
    count_gz = lax.axis_size("gz")
    slots = solutes.shape[3]
    capacity = slots // count_gz
    brick_count = rows // BY * (columns // BX)
    feature = 2 * depth * BY * BX
    bricks = fractions.reshape(2, depth, rows // BY, BY, columns // BX, BX)
    bricks = bricks.transpose(2, 4, 0, 1, 3, 5).reshape(brick_count, feature)
    target = owners.reshape(brick_count)
    onehot = (target[:, None] == jnp.arange(count_gz, dtype=jnp.int32)[None, :]).astype(jnp.float32)
    lower = (jnp.arange(brick_count)[:, None] > jnp.arange(brick_count)[None, :]).astype(
        jnp.float32
    )
    before = jnp.dot(lower, onehot, preferred_element_type=jnp.float32)
    rank = jnp.sum(before * onehot, axis=1).astype(jnp.int32)
    slot_index = target * capacity + rank
    placing = (jnp.arange(slots, dtype=jnp.int32)[:, None] == slot_index[None, :]).astype(
        jnp.bfloat16
    )
    outgoing = jnp.dot(placing, bricks, preferred_element_type=jnp.float32).astype(jnp.bfloat16)
    arrived = lax.all_to_all(outgoing, "gz", split_axis=0, concat_axis=0, tiled=True)
    arrived = arrived.reshape(slots, 2, depth, BY, BX)
    state = solutes.reshape(slots, 2, depth, BY, BX)
    mass = biomass.reshape(slots, depth, BY, BX)
    solutes_next = advance(state, arrived, mass).reshape(solutes.shape)
    return (fractions, solutes_next)


def solution(mesh):
    return jax.shard_map(
        per_device,
        mesh=mesh,
        in_specs=(
            P(("cores", "gz"), "gy", "col"),
            P(),
            P(),
            P(),
            P(),
            P(("cores", "gz"), "gy", "col", None, None),
            P(("cores", "gz"), "gy", "col", None, None, None, None, None),
            P(("cores", "gz"), "gy", "col", None, None, None, None),
        ),
        out_specs=(
            P(None, ("cores", "gz"), "gy", "col"),
            P(("cores", "gz"), "gy", "col", None, None, None, None, None),
        ),
        check_vma=False,
    )
```

profile of v0, /device:TPU:0, one launch (start us, length us, event | category | flops | bytes accessed | tf_op | source)
XLA Modules:
  0.0 125.8 jit_solution(12690100801937874496)
XLA Ops:
  0.6 0.7 fusion.234
  1.4 4.9 %collective-permute-start = (bf16[1,32,256]{2,1,0:T(8,128)(2,1)S(1)}, bf16[1,32,256]{2,1,0:T(8,128)(2,1)S(1)}, u32[]{:S(2)}, u32[]{:S(2)}) collective-permute-start(bf16[1,32,256]{2,1,0:T(8,128)(2,1)S(1)} %get-tuple-element.180), channel_id=1, source_target_pairs={{0,4},{4,8},{8,12},{1,5},{5,9},{9,13},{2,6},{6,10},{10,14},{3,7},{... | collective-permute-start | bytes 49160 | tf_op jit(solution)/shard_map/ppermute | solution.py:18
  6.3 1.3 %collective-permute-start.1 = (bf16[1,32,256]{2,1,0:T(8,128)(2,1)S(1)}, bf16[1,32,256]{2,1,0:T(8,128)(2,1)S(1)}, u32[]{:S(2)}, u32[]{:S(2)}) collective-permute-start(bf16[1,32,256]{2,1,0:T(8,128)(2,1)S(1)} %get-tuple-element.179), channel_id=1, source_target_pairs={{4,0},{8,4},{12,8},{5,1},{9,5},{13,9},{6,2},{10,6},{14,10},{7,3},{... | collective-permute-start | bytes 49160 | tf_op jit(solution)/shard_map/ppermute | solution.py:19
  7.6 0.9 fusion.33
  8.5 1.2 convert_add_fusion
  9.7 1.1 copy.812
  11.3 1.4 %pad_maximum_fusion.3 = (f32[32,6,6,128]{3,2,1,0:T(8,128)}, f32[32,6,6,128]{3,2,1,0:T(8,128)S(1)}) fusion(f32[32,6,1,128]{3,2,1,0:T(1,128)S(1)} %get-tuple-element.126, f32[32,1,4,128]{3,2,1,0:T(4,128)S(1)} %get-tuple-element.142, f32[32,4,4,128]{3,2,1,0:T(4,128)S(1)} %get-tuple-element.108, f32[32,1,4,128]{3,2,1,0:T(4,128)S(1)} %get-tuple-element.141, ...), kind=kLoop, calls=%fused_computation.56 | loop fusion | flops 1179648 | bytes 2359296 | tf_op jit(solution)/shard_map/jit(_pad)/concatenate | solution.py:55
  12.7 0.8 slice_reduce_fusion.12
  13.6 3.4 %collective-permute-start.2 = (bf16[6,1,256]{2,1,0:T(2,128)(2,1)S(1)}, bf16[6,1,256]{2,1,0:T(2,128)(2,1)S(1)}, u32[]{:S(2)}, u32[]{:S(2)}) collective-permute-start(bf16[6,1,256]{2,1,0:T(2,128)(2,1)S(1)} %get-tuple-element.174), channel_id=1, source_target_pairs={{0,2},{1,3},{4,6},{5,7},{8,10},{9,11},{12,14},{13,15},{16,18},{17,... | collective-permute-start | bytes 9224 | tf_op jit(solution)/shard_map/ppermute | solution.py:18
  17.0 1.3 %collective-permute-start.3 = (bf16[6,1,256]{2,1,0:T(2,128)(2,1)S(1)}, bf16[6,1,256]{2,1,0:T(2,128)(2,1)S(1)}, u32[]{:S(2)}, u32[]{:S(2)}) collective-permute-start(bf16[6,1,256]{2,1,0:T(2,128)(2,1)S(1)} %get-tuple-element.175), channel_id=1, source_target_pairs={{2,0},{3,1},{6,4},{7,5},{10,8},{11,9},{14,12},{15,13},{18,16},{19,... | collective-permute-start | bytes 9224 | tf_op jit(solution)/shard_map/ppermute | solution.py:19
  18.3 0.8 slice_reduce_fusion.26
  19.1 0.8 copy.762
  20.6 0.8 copy.771
  21.3 1.2 collective-permute-done.3
  22.7 1.3 %collective-permute-start.4 = (bf16[6,34,1]{2,1,0:T(8,128)(2,1)S(1)}, bf16[6,34,1]{2,1,0:T(8,128)(2,1)S(1)}, u32[]{:S(2)}, u32[]{:S(2)}) collective-permute-start(bf16[6,34,1]{2,1,0:T(8,128)(2,1)S(1)} %get-tuple-element.162), channel_id=1, source_target_pairs={{0,1},{2,3},{4,5},{6,7},{8,9},{10,11},{12,13},{14,15},{16,17},{18,... | collective-permute-start | bytes 1232 | tf_op jit(solution)/shard_map/ppermute | solution.py:18
  24.0 1.3 %collective-permute-start.5 = (bf16[6,34,1]{2,1,0:T(8,128)(2,1)S(1)}, bf16[6,34,1]{2,1,0:T(8,128)(2,1)S(1)}, u32[]{:S(2)}, u32[]{:S(2)}) collective-permute-start(bf16[6,34,1]{2,1,0:T(8,128)(2,1)S(1)} %get-tuple-element.161), channel_id=1, source_target_pairs={{1,0},{3,2},{5,4},{7,6},{9,8},{11,10},{13,12},{15,14},{17,16},{19,... | collective-permute-start | bytes 1232 | tf_op jit(solution)/shard_map/ppermute | solution.py:19
  25.4 0.7 copy.750
  26.1 0.8 copy.756
  26.9 0.7 copy.759
  27.6 0.7 copy.765
  28.3 0.8 copy.768
  29.1 0.7 copy.774
  30.4 0.8 copy.749
  31.1 0.7 copy.751
  31.9 0.8 copy.752
  32.6 0.7 copy.754
  33.4 0.7 copy.755
  34.1 0.8 copy.757
  34.9 0.8 copy.758
  35.6 0.7 copy.760
  36.4 0.7 copy.761
  37.1 0.7 copy.763
  37.9 0.8 copy.764
  38.6 0.7 copy.766
  39.4 0.7 copy.767
  40.1 0.7 copy.769
  40.8 0.8 copy.770
  42.3 0.7 copy.773
  43.1 0.8 copy.775
  43.8 10.8 %stack.120 = bf16[27,4,32,256]{3,0,2,1:T(8,128)(2,1)S(1)} concatenate(bf16[1,4,32,256]{3,0,2,1:T(2,128)(2,1)} %copy.749, bf16[1,4,32,256]{3,0,2,1:T(2,128)(2,1)} %copy.750, bf16[1,4,32,256]{3,0,2,1:T(2,128)(2,1)} %copy.751, bf16[1,4,32,256]{3,0,2,1:T(2,128)(2,1)} %copy.752, bf16[1,4,32,256]{3,0,2,1:T(2,128)(2,1)} %copy.753, bf16[1,4,32,256]{3,0,2,1:T(2,128)(2,1)} %copy.754, ...), dimensions={0} | concatenate | bytes 3538944 | tf_op jit(solution)/shard_map/stack | solution.py:48
  54.7 1.0 fusion.3
  55.8 4.6 %collective-permute-start.6 = (bf16[8,1,32,256]{3,0,2,1:T(8,128)(2,1)S(1)}, bf16[8,1,32,256]{3,0,2,1:T(8,128)(2,1)S(1)}, u32[]{:S(2)}, u32[]{:S(2)}) collective-permute-start(bf16[8,1,32,256]{3,0,2,1:T(8,128)(2,1)S(1)} %get-tuple-element.109), channel_id=1, source_target_pairs={{0,4},{4,8},{8,12},{1,5},{5,9},{9,13},{2,6},{6,10},{10,14},{3,7},{... | collective-permute-start | bytes 393224 | tf_op jit(solution)/shard_map/ppermute | solution.py:18
  60.4 1.3 %collective-permute-start.7 = (bf16[8,1,32,256]{3,0,2,1:T(8,128)(2,1)S(1)}, bf16[8,1,32,256]{3,0,2,1:T(8,128)(2,1)S(1)}, u32[]{:S(2)}, u32[]{:S(2)}) collective-permute-start(bf16[8,1,32,256]{3,0,2,1:T(8,128)(2,1)S(1)} %get-tuple-element.110), channel_id=1, source_target_pairs={{4,0},{8,4},{12,8},{5,1},{9,5},{13,9},{6,2},{10,6},{14,10},{7,3},{... | collective-permute-start | bytes 393224 | tf_op jit(solution)/shard_map/ppermute | solution.py:19
  62.0 2.1 %collective-permute-done.6 = bf16[8,1,32,256]{3,0,2,1:T(8,128)(2,1)S(1)} collective-permute-done((bf16[8,1,32,256]{3,0,2,1:T(8,128)(2,1)S(1)}, bf16[8,1,32,256]{3,0,2,1:T(8,128)(2,1)S(1)}, u32[]{:S(2)}, u32[]{:S(2)}) %collective-permute-start.6) | collective-permute-done | bytes 131104 | tf_op jit(solution)/shard_map/ppermute | solution.py:18
  64.1 4.4 %collective-permute-done.7 = bf16[8,1,32,256]{3,0,2,1:T(8,128)(2,1)S(1)} collective-permute-done((bf16[8,1,32,256]{3,0,2,1:T(8,128)(2,1)S(1)}, bf16[8,1,32,256]{3,0,2,1:T(8,128)(2,1)S(1)}, u32[]{:S(2)}, u32[]{:S(2)}) %collective-permute-start.7) | collective-permute-done | bytes 131104 | tf_op jit(solution)/shard_map/ppermute | solution.py:19
  68.5 3.4 %collective-permute-start.8 = (bf16[8,6,1,256]{3,0,2,1:T(8,128)(2,1)S(1)}, bf16[8,6,1,256]{3,0,2,1:T(8,128)(2,1)S(1)}, u32[]{:S(2)}, u32[]{:S(2)}) collective-permute-start(bf16[8,6,1,256]{3,0,2,1:T(8,128)(2,1)S(1)} %get-tuple-element.105), channel_id=1, source_target_pairs={{0,2},{1,3},{4,6},{5,7},{8,10},{9,11},{12,14},{13,15},{16,18},{17,... | collective-permute-start | bytes 73736 | tf_op jit(solution)/shard_map/ppermute | solution.py:18
  71.9 1.3 %collective-permute-start.9 = (bf16[8,6,1,256]{3,0,2,1:T(8,128)(2,1)S(1)}, bf16[8,6,1,256]{3,0,2,1:T(8,128)(2,1)S(1)}, u32[]{:S(2)}, u32[]{:S(2)}) collective-permute-start(bf16[8,6,1,256]{3,0,2,1:T(8,128)(2,1)S(1)} %get-tuple-element.106), channel_id=1, source_target_pairs={{2,0},{3,1},{6,4},{7,5},{10,8},{11,9},{14,12},{15,13},{18,16},{19,... | collective-permute-start | bytes 73736 | tf_op jit(solution)/shard_map/ppermute | solution.py:19
  73.8 3.8 %collective-permute-done.9 = bf16[8,6,1,256]{3,0,2,1:T(8,128)(2,1)S(1)} collective-permute-done((bf16[8,6,1,256]{3,0,2,1:T(8,128)(2,1)S(1)}, bf16[8,6,1,256]{3,0,2,1:T(8,128)(2,1)S(1)}, u32[]{:S(2)}, u32[]{:S(2)}) %collective-permute-start.9) | collective-permute-done | bytes 24608 | tf_op jit(solution)/shard_map/ppermute | solution.py:19
  78.0 1.3 %collective-permute-start.10 = (bf16[8,6,34,1]{3,0,2,1:T(8,128)(2,1)S(1)}, bf16[8,6,34,1]{3,0,2,1:T(8,128)(2,1)S(1)}, u32[]{:S(2)}, u32[]{:S(2)}) collective-permute-start(bf16[8,6,34,1]{3,0,2,1:T(8,128)(2,1)S(1)} %get-tuple-element.87), channel_id=1, source_target_pairs={{0,1},{2,3},{4,5},{6,7},{8,9},{10,11},{12,13},{14,15},{16,17},{18,... | collective-permute-start | bytes 9800 | tf_op jit(solution)/shard_map/ppermute | solution.py:18
  79.3 1.5 %collective-permute-start.11 = (bf16[8,6,34,1]{3,0,2,1:T(8,128)(2,1)S(1)}, bf16[8,6,34,1]{3,0,2,1:T(8,128)(2,1)S(1)}, u32[]{:S(2)}, u32[]{:S(2)}) collective-permute-start(bf16[8,6,34,1]{3,0,2,1:T(8,128)(2,1)S(1)} %get-tuple-element.88), channel_id=1, source_target_pairs={{1,0},{3,2},{5,4},{7,6},{9,8},{11,10},{13,12},{15,14},{17,16},{19,... | collective-permute-start | bytes 9800 | tf_op jit(solution)/shard_map/ppermute | solution.py:19
  83.3 1.6 %maximum_maximum_fusion = (bf16[8,6,34,257]{3,0,2,1:T(8,128)(2,1)S(1)}, bf16[8,6,34,257]{3,0,2,1:T(8,128)(2,1)S(1)}) fusion(bf16[8,6,1,256]{3,0,2,1:T(8,128)(2,1)S(1)} %collective-permute-done.9, bf16[8,1,32,256]{3,0,2,1:T(8,128)(2,1)S(1)} %collective-permute-done.7, bf16[8,4,32,256]{3,0,2,1:T(8,128)(2,1)S(1)} %fusion.3, ...), kind=kLoop, calls=%fused_computation.5 | loop fusion | flops 10066176 | bytes 2519808 | tf_op jit(solution)/shard_map/concatenate | solution.py:20
  90.4 0.9 fusion.26
  91.3 1.0 fusion.35
  92.6 0.9 fusion
  93.5 3.9 %all-to-all-start = ((bf16[4,8,4096]{2,1,0:T(8,128)(2,1)}), bf16[4,8,4096]{2,1,0:T(8,128)(2,1)S(1)}, u32[]{:S(2)}, u32[]{:S(2)}) async-start(bf16[4,8,4096]{2,1,0:T(8,128)(2,1)} %fusion), calls=%async_computation | async-start | bytes 524288 | tf_op jit(solution)/shard_map/all_to_all | solution.py:106
  97.3 1.1 fusion.222
  98.5 1.4 %fusion.220 = (f32[32,6,6,1]{3,2,1,0:T(8,128)}, f32[32,6,6,1]{3,2,1,0:T(8,128)}) fusion(f32[32,6,6,128]{3,2,1,0:T(8,128)S(1)} %get-tuple-element.191), kind=kLoop, calls=%fused_computation.497 | loop fusion | bytes 18432 | tf_op jit(solution)/shard_map/jit(_pad)/slice | solution.py:55
  100.5 7.0 %all-to-all-done = bf16[4,8,4096]{2,1,0:T(8,128)(2,1)S(1)} async-done(((bf16[4,8,4096]{2,1,0:T(8,128)(2,1)}), bf16[4,8,4096]{2,1,0:T(8,128)(2,1)S(1)}, u32[]{:S(2)}, u32[]{:S(2)}) %all-to-all-start) | async-done | bytes 262176 | tf_op jit(solution)/shard_map/all_to_all | solution.py:106
  107.8 2.3 %fusion.77 = f32[32,4,4,128]{3,2,1,0:T(4,128)S(1)} fusion(f32[32,4,4,128]{3,2,1,0:T(4,128)S(1)} %copy-done.5, f32[32,6,6,1]{3,2,1,0:T(8,128)} %get-tuple-element.104, f32[32,6,1,128]{3,2,1,0:T(1,128)S(1)} %copy-done.17, f32[32,6,1,128]{3,2,1,0:T(1,128)S(1)} %copy-done.15, f32[32,1,4,128]{3,2,1,0:T(4,128)S(1)} %copy-done.13, ...), kind=kLoop, calls=%fused_computation.109 | loop fusion | flops 2818048 | bytes 1778688 | tf_op jit(solution)/shard_map/sub | solution.py:71
  112.0 2.6 %fusion.80 = (f32[32,4,4,128]{3,2,1,0:T(4,128)S(1)}, f32[32,4,4,128]{3,2,1,0:T(4,128)S(1)}) fusion(f32[32,4,4,128]{3,2,1,0:T(4,128)S(1)} %fusion.77, f32[32,6,6,1]{3,2,1,0:T(8,128)S(1)} %get-tuple-element.102, f32[32,6,1,128]{3,2,1,0:T(1,128)S(1)} %get-tuple-element.124, f32[32,6,1,128]{3,2,1,0:T(1,128)S(1)} %get-tuple-element.123, ...), kind=kLoop, calls=%fused_computation.112 | loop fusion | flops 5242880 | bytes 2639872 | tf_op jit(solution)/shard_map/sub | solution.py:71
  116.0 2.7 %fusion.83 = (f32[32,4,4,128]{3,2,1,0:T(4,128)S(1)}, f32[32,4,4,128]{3,2,1,0:T(4,128)S(1)}) fusion(f32[32,4,4,128]{3,2,1,0:T(4,128)S(1)} %get-tuple-element.83, f32[32,6,6,1]{3,2,1,0:T(8,128)S(1)} %get-tuple-element.98, f32[32,6,1,128]{3,2,1,0:T(1,128)S(1)} %get-tuple-element.120, f32[32,6,1,128]{3,2,1,0:T(1,128)S(1)} %get-tuple-element.119, ...), kind=kLoop, calls=%fused_computation.115 | loop fusion | flops 5242880 | bytes 2377728 | tf_op jit(solution)/shard_map/sub | solution.py:71
  120.2 2.7 %fusion.87 = (f32[32,1,4,4,128]{4,3,2,0,1:T(4,128)S(1)}, f32[32,4,4,128]{3,2,1,0:T(4,128)S(1)}) fusion(f32[32,4,4,128]{3,2,1,0:T(4,128)S(1)} %get-tuple-element.81, f32[32,6,6,1]{3,2,1,0:T(8,128)S(1)} %get-tuple-element.94, f32[32,6,1,128]{3,2,1,0:T(1,128)S(1)} %get-tuple-element.116, f32[32,6,1,128]{3,2,1,0:T(1,128)S(1)} %get-tuple-element.115, ...), kind=kLoop, calls=%fused_computation.119 | loop fusion | flops 5242880 | bytes 2377728 | tf_op jit(solution)/shard_map/stack | solution.py:74
  123.6 1.2 fusion.101
  124.9 0.9 copy.780
  (181 shorter events, 18.2 us)
Async XLA Ops:
  0.6 54.1 %copy-start = (bf16[27,8,1]{0,1,2:T(8,128)(2,1)S(1)}, bf16[27,8,1]{0,1,2:T(8,128)(2,1)}, u32[]{:S(2)}) copy-start(bf16[27,8,1]{0,1,2:T(8,128)(2,1)} %param.9) | copy-start | bytes 1300
  1.4 12.1 %collective-permute-start = (bf16[1,32,256]{2,1,0:T(8,128)(2,1)S(1)}, bf16[1,32,256]{2,1,0:T(8,128)(2,1)S(1)}, u32[]{:S(2)}, u32[]{:S(2)}) collective-permute-start(bf16[1,32,256]{2,1,0:T(8,128)(2,1)S(1)} %get-tuple-element.180), channel_id=1, source_target_pairs={{0,4},{4,8},{8,12},{1,5},{5,9},{9,13},{2,6},{6,10},{10,14},{3,7},{... | collective-permute-start | bytes 49160 | tf_op jit(solution)/shard_map/ppermute | solution.py:18
  6.3 7.2 %collective-permute-start.1 = (bf16[1,32,256]{2,1,0:T(8,128)(2,1)S(1)}, bf16[1,32,256]{2,1,0:T(8,128)(2,1)S(1)}, u32[]{:S(2)}, u32[]{:S(2)}) collective-permute-start(bf16[1,32,256]{2,1,0:T(8,128)(2,1)S(1)} %get-tuple-element.179), channel_id=1, source_target_pairs={{4,0},{8,4},{12,8},{5,1},{9,5},{13,9},{6,2},{10,6},{14,10},{7,3},{... | collective-permute-start | bytes 49160 | tf_op jit(solution)/shard_map/ppermute | solution.py:19
  10.8 1.9 %copy-start.2 = (f32[32,4,4,128]{3,2,1,0:T(4,128)}, f32[32,4,4,128]{3,2,1,0:T(4,128)S(1)}, u32[]{:S(2)}) copy-start(f32[32,4,4,128]{3,2,1,0:T(4,128)S(1)} %get-tuple-element.107) | copy-start | bytes 786436
  10.8 1.9 %copy-start.4 = (f32[32,4,4,128]{3,2,1,0:T(4,128)}, f32[32,4,4,128]{3,2,1,0:T(4,128)S(1)}, u32[]{:S(2)}) copy-start(f32[32,4,4,128]{3,2,1,0:T(4,128)S(1)} %get-tuple-element.108) | copy-start | bytes 786436
  10.9 1.8 %copy-start.10 = (f32[32,1,4,128]{3,2,1,0:T(4,128)}, f32[32,1,4,128]{3,2,1,0:T(4,128)S(1)}, u32[]{:S(2)}) copy-start(f32[32,1,4,128]{3,2,1,0:T(4,128)S(1)} %get-tuple-element.141) | copy-start | bytes 196612
  10.9 1.8 %copy-start.12 = (f32[32,1,4,128]{3,2,1,0:T(4,128)}, f32[32,1,4,128]{3,2,1,0:T(4,128)S(1)}, u32[]{:S(2)}) copy-start(f32[32,1,4,128]{3,2,1,0:T(4,128)S(1)} %get-tuple-element.142) | copy-start | bytes 196612
  11.1 1.6 %copy-start.18 = (f32[32,6,1,128]{3,2,1,0:T(1,128)}, f32[32,6,1,128]{3,2,1,0:T(1,128)S(1)}, u32[]{:S(2)}) copy-start(f32[32,6,1,128]{3,2,1,0:T(1,128)S(1)} %get-tuple-element.121) | copy-start | bytes 294916
  11.1 1.6 %copy-start.20 = (f32[32,6,1,128]{3,2,1,0:T(1,128)}, f32[32,6,1,128]{3,2,1,0:T(1,128)S(1)}, u32[]{:S(2)}) copy-start(f32[32,6,1,128]{3,2,1,0:T(1,128)S(1)} %get-tuple-element.122) | copy-start | bytes 294916
  11.1 1.6 %copy-start.9 = (bf16[27,2,8]{0,2,1:T(8,128)(2,1)S(1)}, bf16[27,2,8]{0,2,1:T(8,128)(2,1)}, u32[]{:S(2)}) copy-start(bf16[27,2,8]{0,2,1:T(8,128)(2,1)} %param.11) | copy-start | bytes 2596
  11.1 2.4 %copy-start.22 = (bf16[4,32,256]{2,1,0:T(8,128)(2,1)S(1)}, bf16[4,32,256]{2,1,0:T(8,128)(2,1)}, u32[]{:S(2)}) copy-start(bf16[4,32,256]{2,1,0:T(8,128)(2,1)} %param.8) | copy-start | bytes 196612
  11.3 7.8 %copy-start.14 = (f32[32,6,1,128]{3,2,1,0:T(1,128)}, f32[32,6,1,128]{3,2,1,0:T(1,128)S(1)}, u32[]{:S(2)}) copy-start(f32[32,6,1,128]{3,2,1,0:T(1,128)S(1)} %get-tuple-element.125) | copy-start | bytes 294916
  11.3 7.8 %copy-start.16 = (f32[32,6,1,128]{3,2,1,0:T(1,128)}, f32[32,6,1,128]{3,2,1,0:T(1,128)S(1)}, u32[]{:S(2)}) copy-start(f32[32,6,1,128]{3,2,1,0:T(1,128)S(1)} %get-tuple-element.126) | copy-start | bytes 294916
  13.6 7.7 %collective-permute-start.2 = (bf16[6,1,256]{2,1,0:T(2,128)(2,1)S(1)}, bf16[6,1,256]{2,1,0:T(2,128)(2,1)S(1)}, u32[]{:S(2)}, u32[]{:S(2)}) collective-permute-start(bf16[6,1,256]{2,1,0:T(2,128)(2,1)S(1)} %get-tuple-element.174), channel_id=1, source_target_pairs={{0,2},{1,3},{4,6},{5,7},{8,10},{9,11},{12,14},{13,15},{16,18},{17,... | collective-permute-start | bytes 9224 | tf_op jit(solution)/shard_map/ppermute | solution.py:18
  17.0 5.5 %collective-permute-start.3 = (bf16[6,1,256]{2,1,0:T(2,128)(2,1)S(1)}, bf16[6,1,256]{2,1,0:T(2,128)(2,1)S(1)}, u32[]{:S(2)}, u32[]{:S(2)}) collective-permute-start(bf16[6,1,256]{2,1,0:T(2,128)(2,1)S(1)} %get-tuple-element.175), channel_id=1, source_target_pairs={{2,0},{3,1},{6,4},{7,5},{10,8},{11,9},{14,12},{15,13},{18,16},{19,... | collective-permute-start | bytes 9224 | tf_op jit(solution)/shard_map/ppermute | solution.py:19
  22.7 7.2 %collective-permute-start.4 = (bf16[6,34,1]{2,1,0:T(8,128)(2,1)S(1)}, bf16[6,34,1]{2,1,0:T(8,128)(2,1)S(1)}, u32[]{:S(2)}, u32[]{:S(2)}) collective-permute-start(bf16[6,34,1]{2,1,0:T(8,128)(2,1)S(1)} %get-tuple-element.162), channel_id=1, source_target_pairs={{0,1},{2,3},{4,5},{6,7},{8,9},{10,11},{12,13},{14,15},{16,17},{18,... | collective-permute-start | bytes 1232 | tf_op jit(solution)/shard_map/ppermute | solution.py:18
  24.0 5.9 %collective-permute-start.5 = (bf16[6,34,1]{2,1,0:T(8,128)(2,1)S(1)}, bf16[6,34,1]{2,1,0:T(8,128)(2,1)S(1)}, u32[]{:S(2)}, u32[]{:S(2)}) collective-permute-start(bf16[6,34,1]{2,1,0:T(8,128)(2,1)S(1)} %get-tuple-element.161), channel_id=1, source_target_pairs={{1,0},{3,2},{5,4},{7,6},{9,8},{11,10},{13,12},{15,14},{17,16},{19,... | collective-permute-start | bytes 1232 | tf_op jit(solution)/shard_map/ppermute | solution.py:19
  54.7 7.0 %copy-start.36 = (bf16[2,8]{1,0:T(2,128)(2,1)S(1)}, bf16[2,8]{1,0:T(2,128)(2,1)}, u32[]{:S(2)}) copy-start(bf16[2,8]{1,0:T(2,128)(2,1)} %get-tuple-element.63) | copy-start | bytes 100
  55.8 17.4 %copy-start.47 = (bf16[2,8]{1,0:T(2,128)(2,1)S(1)}, bf16[2,8]{1,0:T(2,128)(2,1)}, u32[]{:S(2)}) copy-start(bf16[2,8]{1,0:T(2,128)(2,1)} %get-tuple-element.73) | copy-start | bytes 100
  55.8 17.7 %copy-start.44 = (bf16[2,8]{1,0:T(2,128)(2,1)S(1)}, bf16[2,8]{1,0:T(2,128)(2,1)}, u32[]{:S(2)}) copy-start(bf16[2,8]{1,0:T(2,128)(2,1)} %get-tuple-element.55) | copy-start | bytes 100
  55.8 8.3 %collective-permute-start.6 = (bf16[8,1,32,256]{3,0,2,1:T(8,128)(2,1)S(1)}, bf16[8,1,32,256]{3,0,2,1:T(8,128)(2,1)S(1)}, u32[]{:S(2)}, u32[]{:S(2)}) collective-permute-start(bf16[8,1,32,256]{3,0,2,1:T(8,128)(2,1)S(1)} %get-tuple-element.109), channel_id=1, source_target_pairs={{0,4},{4,8},{8,12},{1,5},{5,9},{9,13},{2,6},{6,10},{10,14},{3,7},{... | collective-permute-start | bytes 393224 | tf_op jit(solution)/shard_map/ppermute | solution.py:18
  60.4 8.1 %collective-permute-start.7 = (bf16[8,1,32,256]{3,0,2,1:T(8,128)(2,1)S(1)}, bf16[8,1,32,256]{3,0,2,1:T(8,128)(2,1)S(1)}, u32[]{:S(2)}, u32[]{:S(2)}) collective-permute-start(bf16[8,1,32,256]{3,0,2,1:T(8,128)(2,1)S(1)} %get-tuple-element.110), channel_id=1, source_target_pairs={{4,0},{8,4},{12,8},{5,1},{9,5},{13,9},{6,2},{10,6},{14,10},{7,3},{... | collective-permute-start | bytes 393224 | tf_op jit(solution)/shard_map/ppermute | solution.py:19
  68.5 5.3 %collective-permute-start.8 = (bf16[8,6,1,256]{3,0,2,1:T(8,128)(2,1)S(1)}, bf16[8,6,1,256]{3,0,2,1:T(8,128)(2,1)S(1)}, u32[]{:S(2)}, u32[]{:S(2)}) collective-permute-start(bf16[8,6,1,256]{3,0,2,1:T(8,128)(2,1)S(1)} %get-tuple-element.105), channel_id=1, source_target_pairs={{0,2},{1,3},{4,6},{5,7},{8,10},{9,11},{12,14},{13,15},{16,18},{17,... | collective-permute-start | bytes 73736 | tf_op jit(solution)/shard_map/ppermute | solution.py:18
  71.9 5.7 %collective-permute-start.9 = (bf16[8,6,1,256]{3,0,2,1:T(8,128)(2,1)S(1)}, bf16[8,6,1,256]{3,0,2,1:T(8,128)(2,1)S(1)}, u32[]{:S(2)}, u32[]{:S(2)}) collective-permute-start(bf16[8,6,1,256]{3,0,2,1:T(8,128)(2,1)S(1)} %get-tuple-element.106), channel_id=1, source_target_pairs={{2,0},{3,1},{6,4},{7,5},{10,8},{11,9},{14,12},{15,13},{18,16},{19,... | collective-permute-start | bytes 73736 | tf_op jit(solution)/shard_map/ppermute | solution.py:19
  73.8 7.0 %copy-start.46 = (bf16[2,8]{1,0:T(2,128)(2,1)S(1)}, bf16[2,8]{1,0:T(2,128)(2,1)}, u32[]{:S(2)}) copy-start(bf16[2,8]{1,0:T(2,128)(2,1)} %get-tuple-element.76) | copy-start | bytes 100
  77.8 3.3 %copy-start.43 = (bf16[2,8]{1,0:T(2,128)(2,1)S(1)}, bf16[2,8]{1,0:T(2,128)(2,1)}, u32[]{:S(2)}) copy-start(bf16[2,8]{1,0:T(2,128)(2,1)} %get-tuple-element.69) | copy-start | bytes 100
  78.0 5.3 %collective-permute-start.10 = (bf16[8,6,34,1]{3,0,2,1:T(8,128)(2,1)S(1)}, bf16[8,6,34,1]{3,0,2,1:T(8,128)(2,1)S(1)}, u32[]{:S(2)}, u32[]{:S(2)}) collective-permute-start(bf16[8,6,34,1]{3,0,2,1:T(8,128)(2,1)S(1)} %get-tuple-element.87), channel_id=1, source_target_pairs={{0,1},{2,3},{4,5},{6,7},{8,9},{10,11},{12,13},{14,15},{16,17},{18,... | collective-permute-start | bytes 9800 | tf_op jit(solution)/shard_map/ppermute | solution.py:18
  79.3 4.0 %collective-permute-start.11 = (bf16[8,6,34,1]{3,0,2,1:T(8,128)(2,1)S(1)}, bf16[8,6,34,1]{3,0,2,1:T(8,128)(2,1)S(1)}, u32[]{:S(2)}, u32[]{:S(2)}) collective-permute-start(bf16[8,6,34,1]{3,0,2,1:T(8,128)(2,1)S(1)} %get-tuple-element.88), channel_id=1, source_target_pairs={{1,0},{3,2},{5,4},{7,6},{9,8},{11,10},{13,12},{15,14},{17,16},{19,... | collective-permute-start | bytes 9800 | tf_op jit(solution)/shard_map/ppermute | solution.py:19
  81.1 0.7 copy-start.42
  81.4 0.6 copy-start.41
  82.0 0.7 copy-start.40
  82.3 0.6 copy-start.45
  83.3 1.7 %copy-start.31 = (bf16[2,8]{1,0:T(2,128)(2,1)S(1)}, bf16[2,8]{1,0:T(2,128)(2,1)}, u32[]{:S(2)}) copy-start(bf16[2,8]{1,0:T(2,128)(2,1)} %get-tuple-element.64) | copy-start | bytes 100
  83.3 2.0 %copy-start.30 = (bf16[2,8]{1,0:T(2,128)(2,1)S(1)}, bf16[2,8]{1,0:T(2,128)(2,1)}, u32[]{:S(2)}) copy-start(bf16[2,8]{1,0:T(2,128)(2,1)} %get-tuple-element.67) | copy-start | bytes 100
  83.3 2.3 %copy-start.29 = (bf16[2,8]{1,0:T(2,128)(2,1)S(1)}, bf16[2,8]{1,0:T(2,128)(2,1)}, u32[]{:S(2)}) copy-start(bf16[2,8]{1,0:T(2,128)(2,1)} %get-tuple-element.65) | copy-start | bytes 100
  85.0 1.0 copy-start.28
  85.0 1.4 %copy-start.27 = (bf16[2,8]{1,0:T(2,128)(2,1)S(1)}, bf16[2,8]{1,0:T(2,128)(2,1)}, u32[]{:S(2)}) copy-start(bf16[2,8]{1,0:T(2,128)(2,1)} %get-tuple-element.70) | copy-start | bytes 100
  85.3 1.4 %copy-start.35 = (bf16[2,8]{1,0:T(2,128)(2,1)S(1)}, bf16[2,8]{1,0:T(2,128)(2,1)}, u32[]{:S(2)}) copy-start(bf16[2,8]{1,0:T(2,128)(2,1)} %get-tuple-element.72) | copy-start | bytes 100
  85.6 1.4 %copy-start.34 = (bf16[2,8]{1,0:T(2,128)(2,1)S(1)}, bf16[2,8]{1,0:T(2,128)(2,1)}, u32[]{:S(2)}) copy-start(bf16[2,8]{1,0:T(2,128)(2,1)} %get-tuple-element.74) | copy-start | bytes 100
  86.0 1.4 %copy-start.33 = (bf16[2,8]{1,0:T(2,128)(2,1)S(1)}, bf16[2,8]{1,0:T(2,128)(2,1)}, u32[]{:S(2)}) copy-start(bf16[2,8]{1,0:T(2,128)(2,1)} %get-tuple-element.75) | copy-start | bytes 100
  86.4 1.4 %copy-start.26 = (bf16[2,8]{1,0:T(2,128)(2,1)S(1)}, bf16[2,8]{1,0:T(2,128)(2,1)}, u32[]{:S(2)}) copy-start(bf16[2,8]{1,0:T(2,128)(2,1)} %get-tuple-element.53) | copy-start | bytes 100
  86.7 1.4 %copy-start.25 = (bf16[2,8]{1,0:T(2,128)(2,1)S(1)}, bf16[2,8]{1,0:T(2,128)(2,1)}, u32[]{:S(2)}) copy-start(bf16[2,8]{1,0:T(2,128)(2,1)} %get-tuple-element.54) | copy-start | bytes 100
  87.0 1.3 %copy-start.24 = (bf16[2,8]{1,0:T(2,128)(2,1)S(1)}, bf16[2,8]{1,0:T(2,128)(2,1)}, u32[]{:S(2)}) copy-start(bf16[2,8]{1,0:T(2,128)(2,1)} %get-tuple-element.56) | copy-start | bytes 100
  87.4 1.3 %copy-start.23 = (bf16[2,8]{1,0:T(2,128)(2,1)S(1)}, bf16[2,8]{1,0:T(2,128)(2,1)}, u32[]{:S(2)}) copy-start(bf16[2,8]{1,0:T(2,128)(2,1)} %get-tuple-element.57) | copy-start | bytes 100
  88.7 1.3 %copy-start.32 = (bf16[2,8]{1,0:T(2,128)(2,1)S(1)}, bf16[2,8]{1,0:T(2,128)(2,1)}, u32[]{:S(2)}) copy-start(bf16[2,8]{1,0:T(2,128)(2,1)} %get-tuple-element.77) | copy-start | bytes 100
  89.1 1.3 %copy-start.39 = (bf16[2,8]{1,0:T(2,128)(2,1)S(1)}, bf16[2,8]{1,0:T(2,128)(2,1)}, u32[]{:S(2)}) copy-start(bf16[2,8]{1,0:T(2,128)(2,1)} %get-tuple-element.71) | copy-start | bytes 100
  90.4 0.9 copy-start.38
  90.4 0.9 copy-start.48
  91.3 1.2 copy-start.37
  92.3 5.0 %copy-start.1 = (f32[32,6,6,128]{3,2,1,0:T(8,128)S(1)}, f32[32,6,6,128]{3,2,1,0:T(8,128)}, u32[]{:S(2)}) copy-start(f32[32,6,6,128]{3,2,1,0:T(8,128)} %get-tuple-element.190) | copy-start | bytes 1769476
  93.5 14.0 %all-to-all-start = ((bf16[4,8,4096]{2,1,0:T(8,128)(2,1)}), bf16[4,8,4096]{2,1,0:T(8,128)(2,1)S(1)}, u32[]{:S(2)}, u32[]{:S(2)}) async-start(bf16[4,8,4096]{2,1,0:T(8,128)(2,1)} %fusion), calls=%async_computation | async-start | bytes 524288 | tf_op jit(solution)/shard_map/all_to_all | solution.py:106
  98.4 9.2 %copy-start.5 = (f32[32,4,4,128]{3,2,1,0:T(4,128)S(1)}, f32[32,4,4,128]{3,2,1,0:T(4,128)}, u32[]{:S(2)}) copy-start(f32[32,4,4,128]{3,2,1,0:T(4,128)} %copy-done.4) | copy-start | bytes 786436
  98.4 9.3 %copy-start.6 = (bf16[1,1,1,32,4,4,128]{6,5,4,3,2,1,0:T(4,128)(2,1)S(1)}, bf16[1,1,1,32,4,4,128]{6,5,4,3,2,1,0:T(4,128)(2,1)}, u32[]{:S(2)}) copy-start(bf16[1,1,1,32,4,4,128]{6,5,4,3,2,1,0:T(4,128)(2,1)} %param.15) | copy-start | bytes 393220
  98.5 9.3 %copy-start.11 = (f32[32,1,4,128]{3,2,1,0:T(4,128)S(1)}, f32[32,1,4,128]{3,2,1,0:T(4,128)}, u32[]{:S(2)}) copy-start(f32[32,1,4,128]{3,2,1,0:T(4,128)} %copy-done.10) | copy-start | bytes 196612
  98.5 9.3 %copy-start.13 = (f32[32,1,4,128]{3,2,1,0:T(4,128)S(1)}, f32[32,1,4,128]{3,2,1,0:T(4,128)}, u32[]{:S(2)}) copy-start(f32[32,1,4,128]{3,2,1,0:T(4,128)} %copy-done.12) | copy-start | bytes 196612
  98.5 9.3 %copy-start.15 = (f32[32,6,1,128]{3,2,1,0:T(1,128)S(1)}, f32[32,6,1,128]{3,2,1,0:T(1,128)}, u32[]{:S(2)}) copy-start(f32[32,6,1,128]{3,2,1,0:T(1,128)} %copy-done.14) | copy-start | bytes 294916
  98.5 9.3 %copy-start.17 = (f32[32,6,1,128]{3,2,1,0:T(1,128)S(1)}, f32[32,6,1,128]{3,2,1,0:T(1,128)}, u32[]{:S(2)}) copy-start(f32[32,6,1,128]{3,2,1,0:T(1,128)} %copy-done.16) | copy-start | bytes 294916
  110.5 1.0 copy-start.3
  110.5 1.2 copy-start.7
  110.5 1.4 %copy-start.8 = (f32[32,6,6,1]{3,2,1,0:T(8,128)S(1)}, f32[32,6,6,1]{3,2,1,0:T(8,128)}, u32[]{:S(2)}) copy-start(f32[32,6,6,1]{3,2,1,0:T(8,128)} %get-tuple-element.100) | copy-start | bytes 13828
  110.5 1.4 %copy-start.19 = (f32[32,6,1,128]{3,2,1,0:T(1,128)S(1)}, f32[32,6,1,128]{3,2,1,0:T(1,128)}, u32[]{:S(2)}) copy-start(f32[32,6,1,128]{3,2,1,0:T(1,128)} %copy-done.18) | copy-start | bytes 294916
  110.5 1.4 %copy-start.21 = (f32[32,6,1,128]{3,2,1,0:T(1,128)S(1)}, f32[32,6,1,128]{3,2,1,0:T(1,128)}, u32[]{:S(2)}) copy-start(f32[32,6,1,128]{3,2,1,0:T(1,128)} %copy-done.20) | copy-start | bytes 294916
where the time goes:
time: 127 us; the launch traced here: 126 us
  local copies, waits for them, and re-layouts  43.4 us (34%)
  starting transfers between devices  30.6 us (24%)
  other arithmetic  19.1 us (15%)
  waiting for transfers between devices  18.5 us (15%)
  matrix products  12.3 us (10%)
  between operations  1.86 us (1%)
    another operation x29, local copies, waits for them, and re-layouts, single_channel_conv(): stacked = jnp.stack(windows, axis=0)  31.4 us
    ppermute x6, starting transfers between devices, extended(): before = lax.ppermute(last, axis, up)  18.8 us
    dot_general x27, matrix products, conv_layer(): jnp.einsum('oc,czyx->ozyx', weights[offset], window, preferred_element_ty...  9.45 us
    ppermute x6, waiting for transfers between devices, extended(): after = lax.ppermute(initial, axis, down)  9.45 us
    ppermute x6, starting transfers between devices, extended(): after = lax.ppermute(initial, axis, down)  7.93 us
    sub x3, other arithmetic, advance(): carbon_new = carbon + 0.12 * pore * laplace(carbon) + 0.3 * organic - uptake  7.56 us
    all_to_all x1, waiting for transfers between devices, per_device(): lax.all_to_all(outgoing, 'gz', split_axis=0, concat_axis=0, tiled=True)  6.98 us
    unnamed x102, local copies, waits for them, and re-layouts  4.66 us
  transfers between devices with their start and end apart: 13, of which 5 were waited for; matrix products, arithmetic and copies ran while one was open for 15% of the time, Pallas kernels for 0%

commit v1 on v0

v1 whole, which is shorter than its diff:
```python
import functools
import itertools

import jax
import jax.numpy as jnp
from jax import lax
from jax.experimental import pallas as pl
from jax.experimental.pallas import tpu as pltpu
from jax.sharding import PartitionSpec as P

BY = 4
BX = 128
STEPS = 4
MESH = pl.DeviceIdType.MESH
F32 = jnp.float32
BF16 = jnp.bfloat16
AROUND = [d for d in itertools.product((-1, 0, 1), repeat=3) if d != (0, 0, 0)]
PLACE_Z = {0: (0, 4), 1: (4, 2), -1: (6, 2)}
PLACE_Y = {0: (0, 32), 1: (32, 16), -1: (48, 16)}
PLACE_X = {0: (0, 256), 1: (256, 128), -1: (384, 128)}
TAKE_Z = {0: (0, 4), 1: (0, 2), -1: (2, 2)}
TAKE_Y = {0: (0, 32), 1: (0, 16), -1: (16, 16)}
TAKE_X = {0: (0, 256), 1: (0, 128), -1: (128, 128)}
KR = 48
HR = 34
LANES = 384


def region(ref, tables, offset):
    return ref.at[tuple(pl.ds(*table[o]) for table, o in zip(tables, offset))]


def iota(shape, dim):
    return lax.broadcasted_iota(jnp.int32, shape, dim)


def onehot(condition):
    return jnp.where(condition, 1.0, 0.0).astype(BF16)


def dot(a, b):
    return jnp.dot(a, b, preferred_element_type=F32)


def build_first(w1):
    hidden = w1.shape[1]
    rows, cols = hidden * HR, 9 * KR
    i = iota((rows, 1), 0)
    channel, yi = lax.div(i, HR), lax.rem(i, HR)
    expand = onehot(channel == iota((rows, hidden), 1))
    by_row = lax.dot_general(
        expand, w1, (((1,), (1,)), ((), ())), preferred_element_type=F32
    ).astype(BF16)
    j = iota((1, cols), 1)
    tap, r = lax.div(j, KR), lax.rem(j, KR)
    y = jnp.where(r < 40, r, r - KR)
    tap_offset = lax.div(tap, 3) * 9 + lax.rem(tap, 3)
    total = jnp.zeros((rows, cols), F32)
    for dy in range(3):
        pick = onehot(iota((27, cols), 0) == tap_offset + 3 * dy)
        total = total + jnp.where(y == yi + (dy - 2), dot(by_row, pick), 0.0)
    return total.astype(BF16)


def build_second(w2, first_row, last_row):
    hidden = w2.shape[1]
    rows, cols = 192, hidden * HR
    i = iota((rows, 1), 0)
    group, y = lax.div(i, 32), lax.rem(i, 32)
    j = iota((1, cols), 1)
    yi = lax.rem(j, HR)
    inside = jnp.logical_not(((yi == 0) & first_row) | ((yi == HR - 1) & last_row))
    yi = jnp.where(inside, yi, -100)
    pick = onehot(iota((hidden, cols), 0) == lax.div(j, HR))
    blocks = []
    for dz in range(3):
        total = jnp.zeros((rows, cols), F32)
        for dy in range(3):
            select = onehot(iota((rows, 54), 1) == (9 * dz + 3 * dy) * 2 + group)
            values = dot(dot(select, w2).astype(BF16), pick)
            total = total + jnp.where(yi == y + dy, values, 0.0)
        blocks.append(total.astype(BF16))
    return blocks


def build_placing(owners_ref, slots, capacity):
    count = owners_ref.shape[0]
    target = [owners_ref[b] for b in range(count)]
    j = iota((1, 128), 1)
    brick = ((j & 31) >> 2) * 2 + (j >> 6)
    slot = jnp.zeros((1, 128), jnp.int32)
    for b in range(count):
        rank = jnp.int32(0)
        for other in range(b):
            rank = rank + jnp.where(target[other] == target[b], 1, 0)
        slot = jnp.where(brick == b, target[b] * capacity + rank, slot)
    column = slot * 8 + ((j >> 5) & 1) * 4 + (j & 3)
    i = iota((slots * 8, 1), 0)
    owner = lax.div(i, capacity * 8)
    row = (owner * capacity + lax.rem(i, capacity)) * 8 + lax.rem(lax.div(i, capacity), 8)
    return onehot(row == column)


def diffuse(carbon, oxygen, pore, organic, mass, lane):
    low, high = lane == 0, lane == BX - 1
    pore_c = [0.12 * v for v in pore]
    pore_o = [0.16 * v for v in pore]
    gain = [0.3 * v for v in organic]
    mass = [0.25 * v for v in mass]

    def laplace(field, q):
        z, y = q // 4, q % 4
        v = field[q]
        total = jnp.where(low, v, pltpu.roll(v, 1, 1)) + jnp.where(high, v, pltpu.roll(v, BX - 1, 1))
        near = 2
        for ok, at in ((z > 0, q - 4), (z < 3, q + 4), (y > 0, q - 1), (y < 3, q + 1)):
            if ok:
                total = total + field[at]
                near += 1
        return total - float(near) * v

    for _ in range(STEPS):
        carbon_new, oxygen_new = [], []
        for q in range(16):
            c, o = carbon[q], oxygen[q]
            uptake = mass[q] * c * o / ((0.5 + jnp.abs(c)) * (0.3 + jnp.abs(o)))
            carbon_new.append(c + pore_c[q] * laplace(carbon, q) + gain[q] - uptake)
            oxygen_new.append(o + pore_o[q] * laplace(oxygen, q) - uptake)
        carbon, oxygen = carbon_new, oxygen_new
    return carbon, oxygen


def kernel(
    sizes, capacity,
    density, w1_ref, b1_ref, w2_ref, b2_ref, owners_ref, solutes, biomass,
    fractions, solutes_next,
    tile, first, second, shifted, hidden, frac, out, arrived, state, state_new, mass_in, mass, gathered,
    halo_send, halo_recv, brick_send, brick_recv, local_sem, group_sem,
):
    n, n_gy, n_col = sizes
    slots = n * capacity
    here = (lax.axis_index("gz"), lax.axis_index("gy"), lax.axis_index("col"))
    me = here[0]

    def exists(offset):
        ok = None
        for position, size, o in zip(here, sizes, offset):
            test = None if o == 0 else (position + o >= 0) & (position + o < size)
            ok = test if ok is None else ok if test is None else ok & test
        return ok

    def device(offset):
        return {"gz": here[0] + offset[0], "gy": here[1] + offset[1], "col": here[2] + offset[2]}

    def halo(offset, index, receiver):
        seen = tuple(-o for o in offset) if not receiver else offset
        return pltpu.make_async_remote_copy(
            src_ref=region(density, (TAKE_Z, TAKE_Y, TAKE_X), seen),
            dst_ref=region(tile, (PLACE_Z, PLACE_Y, PLACE_X), seen),
            send_sem=halo_send.at[index],
            recv_sem=halo_recv.at[AROUND.index(seen)],
            device_id=device(offset),
            device_id_type=MESH,
        )

    tile[...] = jnp.zeros_like(tile)
    barrier = pltpu.get_barrier_semaphore()
    expected = jnp.int32(n - 1)
    for offset in AROUND:
        ok = exists(offset)
        expected = expected + jnp.where(ok, 1, 0)

        @pl.when(ok)
        def _():
            pl.semaphore_signal(barrier, inc=1, device_id=device(offset), device_id_type=MESH)

    for j in range(1, n):
        pl.semaphore_signal(
            barrier, inc=1, device_id={"gz": lax.rem(me + j, n)}, device_id_type=MESH
        )
    own = pltpu.make_async_copy(
        density, region(tile, (PLACE_Z, PLACE_Y, PLACE_X), (0, 0, 0)), local_sem.at[0]
    )
    own.start()
    load_state = pltpu.make_async_copy(solutes, state, local_sem.at[1])
    load_mass = pltpu.make_async_copy(biomass, mass_in, local_sem.at[2])
    pl.semaphore_wait(barrier, expected)

    for index, offset in enumerate(AROUND):

        @pl.when(exists(offset))
        def _():
            halo(offset, index, False).start()

    load_state.start()
    load_mass.start()

    first[...] = build_first(w1_ref[...])
    for dz, block in enumerate(build_second(w2_ref[...], here[1] == 0, here[1] == n_gy - 1)):
        second[dz] = block
    placing = build_placing(owners_ref, slots, capacity)
    channel = lax.div(iota((272, 1), 0), HR)
    bias1 = jnp.zeros((272, 1), F32)
    for o in range(8):
        bias1 = jnp.where(channel == o, b1_ref[o], bias1)
    bias2 = jnp.where(iota((64, 1), 0) < 32, b2_ref[0], b2_ref[1])
    lane = iota((1, BX), 1)
    keep = jnp.where(
        ((lane == 0) & (here[2] < n_col - 1)) | ((lane == BX - 1) & (here[2] > 0)), 1.0, 0.0
    )
    load_mass.wait()
    for g in range(slots // 8):
        mass[g] = mass_in[g].astype(F32)

    own.wait()
    for index, offset in enumerate(AROUND):

        @pl.when(exists(offset))
        def _():
            halo(offset, index, True).wait_recv()

    half_row = iota((16, 512), 0) < 8
    half_lane = iota((KR, BX), 1) < 64
    for zz in range(8):
        z = (zz + 6) % 8
        side = jnp.where(half_row, tile[z, 32:48, :].astype(F32), tile[z, 48:64, :].astype(F32))
        whole = jnp.concatenate([tile[z, 0:32, :].astype(F32), side], axis=0)
        edge = jnp.where(half_lane, whole[:, 256:384], whole[:, 384:512])
        whole = jnp.concatenate([whole[:, :256], edge], axis=1)
        base = zz * 3 * KR
        shifted[base : base + KR, :] = pltpu.roll(whole, 1, 1).astype(BF16)
        shifted[base + KR : base + 2 * KR, :] = whole.astype(BF16)
        shifted[base + 2 * KR : base + 3 * KR, :] = pltpu.roll(whole, LANES - 1, 1).astype(BF16)

    def hidden_slice(zi):
        value = dot(first[...], shifted[zi * 3 * KR : (zi + 3) * 3 * KR, :])
        value = jnp.maximum(value + bias1, 0.0)
        hidden[zi, :, 0:256] = value[:, :256].astype(BF16)
        hidden[zi, :, 256:384] = (value[:, 256:] * keep).astype(BF16)

    def brick_copy(j, z):
        to = lax.rem(me + j, n)
        return pltpu.make_async_remote_copy(
            src_ref=out.at[to, z],
            dst_ref=arrived.at[me, z],
            send_sem=brick_send.at[j, z],
            recv_sem=brick_recv.at[j, z],
            device_id={"gz": to},
            device_id_type=MESH,
        )

    hidden_slice(0)

    @pl.when(me == 0)
    def _():
        hidden[0] = jnp.zeros_like(hidden[0])

    hidden_slice(1)
    per = 8 * capacity
    for z in range(4):
        hidden_slice(z + 2)
        if z == 3:

            @pl.when(me == n - 1)
            def _():
                hidden[5] = jnp.zeros_like(hidden[5])

        total = jnp.zeros((192, LANES), F32)
        for dz in range(3):
            total = total + dot(second[dz], hidden[z + dz])
        value = (
            pltpu.roll(total[0:64], 1, 1) + total[64:128] + pltpu.roll(total[128:192], LANES - 1, 1)
        )[:, :256]
        value = (1.0 / (1.0 + jnp.exp(-(value + bias2)))).astype(BF16)
        frac[0, z] = value[:32]
        frac[1, z] = value[32:]
        placed = dot(placing, jnp.concatenate([value[:, :128], value[:, 128:]], axis=0)).astype(BF16)
        for d in range(n):
            out[d, z] = placed[d * per : (d + 1) * per]
        for j in range(1, n):
            brick_copy(j, z).start()
    store_frac = pltpu.make_async_copy(frac, fractions, local_sem.at[3])
    store_frac.start()

    load_state.wait()

    def received(j, z):
        source = lax.rem(me - j + n, n)
        pltpu.make_async_remote_copy(
            src_ref=out.at[source, z],
            dst_ref=arrived.at[source, z],
            send_sem=brick_send.at[j, z],
            recv_sem=brick_recv.at[j, z],
            device_id={"gz": source},
            device_id_type=MESH,
        ).wait_recv()

    def group_copy(g):
        return pltpu.make_async_copy(state_new.at[g], solutes_next.at[g], group_sem.at[g])

    def group(g, pore, organic):
        carbon = [state[g, pl.ds(q, 8, stride=32), :] for q in range(16)]
        oxygen = [state[g, pl.ds(16 + q, 8, stride=32), :] for q in range(16)]
        held = [mass[g, pl.ds(q, 8, stride=16), :] for q in range(16)]
        carbon, oxygen = diffuse(carbon, oxygen, pore, organic, held, iota((8, BX), 1))
        for q in range(16):
            state_new[g, pl.ds(q, 8, stride=32), :] = carbon[q]
            state_new[g, pl.ds(16 + q, 8, stride=32), :] = oxygen[q]
        group_copy(g).start()

    if capacity == 8:
        for j in range(n):
            source = lax.rem(me - j + n, n)
            values = [[None] * 16, [None] * 16]
            for z in range(4):
                if j:
                    received(j, z)
                ref = arrived if j else out
                for o in range(2):
                    for pair in range(2):
                        at = o * 32 + pair * 16
                        both = ref[source, z, at : at + 16, :].astype(F32)
                        values[o][z * 4 + pair * 2] = both[:8]
                        values[o][z * 4 + pair * 2 + 1] = both[8:]
            group(source, *values)
    else:
        for z in range(4):
            arrived[me, z] = out[me, z]
        for j in range(1, n):
            for z in range(4):
                received(j, z)
        for s in range(n):
            for z in range(4):
                block = arrived[s, z].astype(F32)
                for o in range(2):
                    for y in range(4):
                        at = (o * 4 + y) * capacity
                        gathered[o * 16 + z * 4 + y, s * capacity : (s + 1) * capacity, :] = block[
                            at : at + capacity
                        ]

        @pl.loop(0, slots // 8)
        def _(g):
            start = pl.multiple_of(g * 8, 8)
            group(
                g,
                [gathered[q, pl.ds(start, 8), :] for q in range(16)],
                [gathered[16 + q, pl.ds(start, 8), :] for q in range(16)],
            )

    for index, offset in enumerate(AROUND):

        @pl.when(exists(offset))
        def _():
            halo(offset, index, False).wait_send()

    for j in range(1, n):
        for z in range(4):
            brick_copy(j, z).wait_send()
    store_frac.wait()
    for g in range(slots // 8):
        group_copy(g).wait()


def per_device(
    sizes, density, first_kernel, first_bias, second_kernel, second_bias, owners, solutes, biomass
):
    n = sizes[0]
    slots = solutes.shape[3]
    capacity = slots // n
    per = 8 * capacity
    vmem, smem = pl.BlockSpec(memory_space=pltpu.VMEM), pl.BlockSpec(memory_space=pltpu.SMEM)
    anywhere = pl.BlockSpec(memory_space=pl.ANY)
    groups = slots // 8
    fractions, solutes_next = pl.pallas_call(
        functools.partial(kernel, sizes, capacity),
        out_shape=(
            jax.ShapeDtypeStruct((2,) + density.shape, BF16),
            jax.ShapeDtypeStruct((groups, 256, BX), F32),
        ),
        in_specs=[anywhere, vmem, smem, vmem, smem, smem, anywhere, anywhere],
        out_specs=(anywhere, anywhere),
        scratch_shapes=[
            pltpu.VMEM((8, 64, 512), BF16),
            pltpu.VMEM((272, 9 * KR), BF16),
            pltpu.VMEM((3, 192, 272), BF16),
            pltpu.VMEM((8 * 3 * KR, LANES), BF16),
            pltpu.VMEM((6, 272, LANES), BF16),
            pltpu.VMEM((2,) + density.shape, BF16),
            pltpu.VMEM((n, 4, per, BX), BF16),
            pltpu.VMEM((n, 4, per, BX), BF16),
            pltpu.VMEM((groups, 256, BX), F32),
            pltpu.VMEM((groups, 256, BX), F32),
            pltpu.VMEM((groups, 128, BX), BF16),
            pltpu.VMEM((groups, 128, BX), F32),
            pltpu.VMEM((32, slots if capacity != 8 else 8, BX), F32),
            pltpu.SemaphoreType.DMA((26,)),
            pltpu.SemaphoreType.DMA((26,)),
            pltpu.SemaphoreType.DMA((n, 4)),
            pltpu.SemaphoreType.DMA((n, 4)),
            pltpu.SemaphoreType.DMA((4,)),
            pltpu.SemaphoreType.DMA((groups,)),
        ],
        compiler_params=pltpu.CompilerParams(
            collective_id=0, has_side_effects=True, vmem_limit_bytes=32 * 1024 * 1024
        ),
    )(
        density,
        first_kernel.reshape(27, 8),
        first_bias,
        second_kernel.reshape(54, 8),
        second_bias,
        owners.reshape(-1),
        solutes.reshape(groups, 256, BX),
        biomass.reshape(groups, 128, BX),
    )
    return fractions, solutes_next.reshape(solutes.shape)


def solution(mesh):
    sizes = tuple(mesh.shape[axis] for axis in ("gz", "gy", "col"))
    return jax.shard_map(
        functools.partial(per_device, sizes),
        mesh=mesh,
        in_specs=(
            P(("cores", "gz"), "gy", "col"),
            P(),
            P(),
            P(),
            P(),
            P(("cores", "gz"), "gy", "col", None, None),
            P(("cores", "gz"), "gy", "col", None, None, None, None, None),
            P(("cores", "gz"), "gy", "col", None, None, None, None),
        ),
        out_specs=(
            P(None, ("cores", "gz"), "gy", "col"),
            P(("cores", "gz"), "gy", "col", None, None, None, None, None),
        ),
        check_vma=False,
    )
```

time: 127 us -> 27.9 us (0.22)
  local copies, waits for them, and re-layouts: 43.4 us -> 6.37 us
  starting transfers between devices: 30.6 us -> 0 us
  Pallas kernels: 0 us -> 20.6 us
  other arithmetic: 19.1 us -> 0 us
  waiting for transfers between devices: 18.5 us -> 0 us
  matrix products: 12.3 us -> 0 us
    another operation x29 -> x0, local copies, waits for them, and re-layouts: 31.4 us -> none  [single_channel_conv(): stacked = jnp.stack(windows, axis=0)]
    ppermute x12 -> x0, starting transfers between devices: 26.8 us -> none  [the longest x6 18.8 us: extended(): before = lax.ppermute(last, axis, up)]
    pallas_call x0 -> x1, Pallas kernels: none -> 20.6 us  [per_device(): pl.pallas_call(functools.partial(kernel, sizes, capacity), out_shape=(jax...]
    dot_general x30 -> x0, matrix products: 12.3 us -> none  [the longest x27 9.45 us: conv_layer(): jnp.einsum('oc,czyx->ozyx', weights[offset], window, preferred_element_ty...]
    ppermute x12 -> x0, waiting for transfers between devices: 11.6 us -> none  [the longest x6 9.45 us: extended(): after = lax.ppermute(initial, axis, down)]
    sub x3 -> x0, other arithmetic: 7.56 us -> none  [advance(): carbon_new = carbon + 0.12 * pore * laplace(carbon) + 0.3 * organic - uptake]
    all_to_all x1 -> x0, waiting for transfers between devices: 6.98 us -> none  [per_device(): lax.all_to_all(outgoing, 'gz', split_axis=0, concat_axis=0, tiled=True)]
    slice x23 -> x0, local copies, waits for them, and re-layouts: 6.95 us -> none  [the longest x16 4.31 us: laplace(): jnp.pad(field, [(0, 0)] * (field.ndim - 3) + [(1, 1), (1, 1), (1, 1)], mo...]
  transfers between devices with their start and end apart: 13 -> 0, of which waited for: 5 -> 0; matrix products, arithmetic and copies ran while one was open for 15% -> 0% of each run, Pallas kernels for 0% -> 0%
where the time goes in v1:
time: 27.9 us; the launch traced here: 27.6 us
  Pallas kernels  20.6 us (74%)
  local copies, waits for them, and re-layouts  6.37 us (23%)
  between operations  0.68 us (2%)
    pallas_call x1, Pallas kernels, per_device(): pl.pallas_call(functools.partial(kernel, sizes, capacity), out_shape=(jax...  20.6 us
    unnamed x20, local copies, waits for them, and re-layouts  6.34 us

profile of v1, /device:TPU:0, one launch (start us, length us, event | category | flops | bytes accessed | tf_op | source)
XLA Modules:
  0.0 27.6 jit_solution(4546969701047368812)
XLA Ops:
  0.6 0.0 copy-start.7
  0.6 0.7 %copy-done.7 = bf16[27,8,1]{0,1,2:T(8,128)(2,1)S(1)} copy-done((bf16[27,8,1]{0,1,2:T(8,128)(2,1)S(1)}, bf16[27,8,1]{0,1,2:T(8,128)(2,1)}, u32[]{:S(2)}) %copy-start.7) | copy-done | bytes 456
  1.3 0.0 copy-start.6
  1.3 0.1 copy.12
  1.4 0.6 %copy-done.6 = bf16[27,2,8]{0,2,1:T(8,128)(2,1)S(1)} copy-done((bf16[27,2,8]{0,2,1:T(8,128)(2,1)S(1)}, bf16[27,2,8]{0,2,1:T(8,128)(2,1)}, u32[]{:S(2)}) %copy-start.6) | copy-done | bytes 888
  2.0 0.1 copy.13
  2.1 0.0 copy-start.3
  2.1 0.0 copy-start.4
  2.1 0.0 copy-start.5
  2.2 0.6 %copy-done.3 = f32[8]{0:T(128)S(1)} copy-done((f32[8]{0:T(128)S(1)}, f32[8]{0:T(128)}, u32[]{:S(2)}) %copy-start.3) | copy-done | bytes 56
  2.8 0.0 copy-done.4
  2.8 0.0 copy-done.5
  2.8 0.0 copy-start
  2.8 1.0 %copy-done = f32[1,1,1,32,2,4,4,128]{7,6,5,4,3,2,1,0:T(4,128)S(1)} copy-done((f32[1,1,1,32,2,4,4,128]{7,6,5,4,3,2,1,0:T(4,128)S(1)}, f32[1,1,1,32,2,4,4,128]{7,6,5,4,3,2,1,0:T(4,128)}, u32[]{:S(2)}) %copy-start) | copy-done | bytes 524312
  3.8 0.0 copy-start.1
  3.8 0.9 %copy-done.1 = bf16[1,1,1,32,4,4,128]{6,5,4,3,2,1,0:T(4,128)(2,1)S(1)} copy-done((bf16[1,1,1,32,4,4,128]{6,5,4,3,2,1,0:T(4,128)(2,1)S(1)}, bf16[1,1,1,32,4,4,128]{6,5,4,3,2,1,0:T(4,128)(2,1)}, u32[]{:S(2)}) %copy-start.1) | copy-done | bytes 131096
  4.7 0.0 copy-start.2
  4.7 0.8 %copy-done.2 = bf16[4,32,256]{2,1,0:T(8,128)(2,1)S(1)} copy-done((bf16[4,32,256]{2,1,0:T(8,128)(2,1)S(1)}, bf16[4,32,256]{2,1,0:T(8,128)(2,1)}, u32[]{:S(2)}) %copy-start.2) | copy-done | bytes 65560
  5.6 20.6 %shard_map.95 = (bf16[2,4,32,256]{3,2,1,0:T(8,128)(2,1)S(1)}, f32[4,256,128]{2,1,0:T(8,128)S(1)}) custom-call(bf16[4,32,256]{2,1,0:T(8,128)(2,1)S(1)} %copy-done.2, bf16[27,8]{1,0:T(8,128)(2,1)S(1)} %bitcast.8, f32[8]{0:T(128)S(1)} %copy-done.3, bf16[54,8]{1,0:T(8,128)(2,1)S(1)} %reshape.23.w2_ref, f32[2]{0:T(128)S(1)} %copy-done.4, s32[16]{0:T(128)S(1)} %bitcast.9, ...), custom_call_target="tpu_custom_call" | custom-call | tf_op jit(solution)/shard_map/pallas_call | solution.py:375
  26.2 0.7 %copy.16 = bf16[2,4,32,256]{3,2,1,0:T(8,128)(2,1)} copy(bf16[2,4,32,256]{3,2,1,0:T(8,128)(2,1)S(1)} %get-tuple-element.8) | data formatting | bytes 262144
  26.9 0.8 %copy.17 = f32[1,1,1,32,2,4,4,128]{7,6,5,4,3,2,1,0:T(4,128)} copy(f32[1,1,1,32,2,4,4,128]{7,6,5,4,3,2,1,0:T(4,128)S(1)} %bitcast.6) | data formatting | bytes 1048576
  (1 shorter events, 0.0 us)
Async XLA Ops:
  0.6 0.7 %copy-start.7 = (bf16[27,8,1]{0,1,2:T(8,128)(2,1)S(1)}, bf16[27,8,1]{0,1,2:T(8,128)(2,1)}, u32[]{:S(2)}) copy-start(bf16[27,8,1]{0,1,2:T(8,128)(2,1)} %param.9) | copy-start | bytes 1300
  1.3 0.7 %copy-start.6 = (bf16[27,2,8]{0,2,1:T(8,128)(2,1)S(1)}, bf16[27,2,8]{0,2,1:T(8,128)(2,1)}, u32[]{:S(2)}) copy-start(bf16[27,2,8]{0,2,1:T(8,128)(2,1)} %param.11) | copy-start | bytes 2596
  2.1 0.7 %copy-start.3 = (f32[8]{0:T(128)S(1)}, f32[8]{0:T(128)}, u32[]{:S(2)}) copy-start(f32[8]{0:T(128)} %b1_ref.1) | copy-start | bytes 100
  2.1 0.7 %copy-start.4 = (f32[2]{0:T(128)S(1)}, f32[2]{0:T(128)}, u32[]{:S(2)}) copy-start(f32[2]{0:T(128)} %b2_ref.1) | copy-start | bytes 28
  2.1 0.7 %copy-start.5 = (s32[1,1,1,16,1]{3,4,2,1,0:T(1,128)S(1)}, s32[1,1,1,16,1]{3,4,2,1,0:T(1,128)}, u32[]{:S(2)}) copy-start(s32[1,1,1,16,1]{3,4,2,1,0:T(1,128)} %param.13) | copy-start | bytes 196
  2.8 1.0 %copy-start = (f32[1,1,1,32,2,4,4,128]{7,6,5,4,3,2,1,0:T(4,128)S(1)}, f32[1,1,1,32,2,4,4,128]{7,6,5,4,3,2,1,0:T(4,128)}, u32[]{:S(2)}) copy-start(f32[1,1,1,32,2,4,4,128]{7,6,5,4,3,2,1,0:T(4,128)} %param.14) | copy-start | bytes 1572868
  3.8 0.9 %copy-start.1 = (bf16[1,1,1,32,4,4,128]{6,5,4,3,2,1,0:T(4,128)(2,1)S(1)}, bf16[1,1,1,32,4,4,128]{6,5,4,3,2,1,0:T(4,128)(2,1)}, u32[]{:S(2)}) copy-start(bf16[1,1,1,32,4,4,128]{6,5,4,3,2,1,0:T(4,128)(2,1)} %param.15) | copy-start | bytes 393220
  4.7 0.8 %copy-start.2 = (bf16[4,32,256]{2,1,0:T(8,128)(2,1)S(1)}, bf16[4,32,256]{2,1,0:T(8,128)(2,1)}, u32[]{:S(2)}) copy-start(bf16[4,32,256]{2,1,0:T(8,128)(2,1)} %density.1) | copy-start | bytes 196612

commit v2 on v1

--- a/solution.py
+++ b/solution.py
@@ -43,14 +43,12 @@
 
 
 def build_first(w1):
-    hidden = w1.shape[1]
+    hidden = w1.shape[0]
     rows, cols = hidden * HR, 9 * KR
     i = iota((rows, 1), 0)
     channel, yi = lax.div(i, HR), lax.rem(i, HR)
     expand = onehot(channel == iota((rows, hidden), 1))
-    by_row = lax.dot_general(
-        expand, w1, (((1,), (1,)), ((), ())), preferred_element_type=F32
-    ).astype(BF16)
+    by_row = dot(expand, w1).astype(BF16)
     j = iota((1, cols), 1)
     tap, r = lax.div(j, KR), lax.rem(j, KR)
     y = jnp.where(r < 40, r, r - KR)
@@ -63,7 +61,7 @@
 
 
 def build_second(w2, first_row, last_row):
-    hidden = w2.shape[1]
+    hidden = w2.shape[0] // 2
     rows, cols = 192, hidden * HR
     i = iota((rows, 1), 0)
     group, y = lax.div(i, 32), lax.rem(i, 32)
@@ -71,13 +69,17 @@
     yi = lax.rem(j, HR)
     inside = jnp.logical_not(((yi == 0) & first_row) | ((yi == HR - 1) & last_row))
     yi = jnp.where(inside, yi, -100)
-    pick = onehot(iota((hidden, cols), 0) == lax.div(j, HR))
+    pick = onehot(lax.rem(iota((2 * hidden, cols), 0), hidden) == lax.div(j, HR))
+    same = lax.rem(group, 2) == lax.div(iota((1, 2 * hidden), 1), hidden)
     blocks = []
     for dz in range(3):
         total = jnp.zeros((rows, cols), F32)
         for dy in range(3):
-            select = onehot(iota((rows, 54), 1) == (9 * dz + 3 * dy) * 2 + group)
-            values = dot(dot(select, w2).astype(BF16), pick)
+            select = onehot(iota((rows, 27), 1) == 9 * dz + 3 * dy + lax.div(group, 2))
+            values = lax.dot_general(
+                select, w2, (((1,), (1,)), ((), ())), preferred_element_type=F32
+            )
+            values = dot(jnp.where(same, values, 0.0).astype(BF16), pick)
             total = total + jnp.where(yi == y + dy, values, 0.0)
         blocks.append(total.astype(BF16))
     return blocks
@@ -132,9 +134,9 @@
 
 def kernel(
     sizes, capacity,
-    density, w1_ref, b1_ref, w2_ref, b2_ref, owners_ref, solutes, biomass,
+    density, w1_hbm, b1_hbm, w2_hbm, b2_hbm, owners_hbm, solutes, biomass,
     fractions, solutes_next,
-    tile, first, second, shifted, hidden, frac, out, arrived, state, state_new, mass_in, mass, gathered,
+    w1_ref, b1_ref, w2_ref, b2_ref, owners_ref, tile, first, second, shifted, hidden, frac, out, arrived, state, state_new, mass_in, mass, gathered,
     halo_send, halo_recv, brick_send, brick_recv, local_sem, group_sem,
 ):
     n, n_gy, n_col = sizes
@@ -163,6 +165,17 @@
             device_id_type=MESH,
         )
 
+    small = [
+        pltpu.make_async_copy(source, target, local_sem.at[4 + i])
+        for i, (source, target) in enumerate(
+            (
+                (w1_hbm, w1_ref), (w2_hbm, w2_ref), (b1_hbm, b1_ref), (b2_hbm, b2_ref),
+                (owners_hbm, owners_ref),
+            )
+        )
+    ]
+    for copy in small:
+        copy.start()
     tile[...] = jnp.zeros_like(tile)
     barrier = pltpu.get_barrier_semaphore()
     expected = jnp.int32(n - 1)
@@ -195,6 +208,8 @@
     load_state.start()
     load_mass.start()
 
+    for copy in small:
+        copy.wait()
     first[...] = build_first(w1_ref[...])
     for dz, block in enumerate(build_second(w2_ref[...], here[1] == 0, here[1] == n_gy - 1)):
         second[dz] = block
@@ -369,8 +384,7 @@
     slots = solutes.shape[3]
     capacity = slots // n
     per = 8 * capacity
-    vmem, smem = pl.BlockSpec(memory_space=pltpu.VMEM), pl.BlockSpec(memory_space=pltpu.SMEM)
-    anywhere = pl.BlockSpec(memory_space=pl.ANY)
+    anywhere = pl.BlockSpec(memory_space=pltpu.HBM)
     groups = slots // 8
     fractions, solutes_next = pl.pallas_call(
         functools.partial(kernel, sizes, capacity),
@@ -378,9 +392,14 @@
             jax.ShapeDtypeStruct((2,) + density.shape, BF16),
             jax.ShapeDtypeStruct((groups, 256, BX), F32),
         ),
-        in_specs=[anywhere, vmem, smem, vmem, smem, smem, anywhere, anywhere],
+        in_specs=[anywhere] * 8,
         out_specs=(anywhere, anywhere),
         scratch_shapes=[
+            pltpu.VMEM((8, 27), BF16),
+            pltpu.SMEM((8,), F32),
+            pltpu.VMEM((16, 27), BF16),
+            pltpu.SMEM((2,), F32),
+            pltpu.SMEM((16,), jnp.int32),
             pltpu.VMEM((8, 64, 512), BF16),
             pltpu.VMEM((272, 9 * KR), BF16),
             pltpu.VMEM((3, 192, 272), BF16),
@@ -398,17 +417,17 @@
             pltpu.SemaphoreType.DMA((26,)),
             pltpu.SemaphoreType.DMA((n, 4)),
             pltpu.SemaphoreType.DMA((n, 4)),
-            pltpu.SemaphoreType.DMA((4,)),
+            pltpu.SemaphoreType.DMA((9,)),
             pltpu.SemaphoreType.DMA((groups,)),
         ],
         compiler_params=pltpu.CompilerParams(
-            collective_id=0, has_side_effects=True, vmem_limit_bytes=32 * 1024 * 1024
+            collective_id=0, has_side_effects=True, vmem_limit_bytes=64 * 1024 * 1024
         ),
     )(
         density,
-        first_kernel.reshape(27, 8),
+        first_kernel.transpose(2, 1, 0).reshape(8, 27),
         first_bias,
-        second_kernel.reshape(54, 8),
+        second_kernel.transpose(1, 2, 0).reshape(16, 27),
         second_bias,
         owners.reshape(-1),
         solutes.reshape(groups, 256, BX),

time: 27.9 us -> 24.9 us (0.89)
  local copies, waits for them, and re-layouts: 6.37 us -> 3.44 us
    unnamed x20 -> x2, local copies, waits for them, and re-layouts: 6.34 us -> 3.44 us
where the time goes in v2:
time: 24.9 us; the launch traced here: 24.7 us
  Pallas kernels  20.6 us (83%)
  local copies, waits for them, and re-layouts  3.44 us (14%)
  between operations  0.64 us (3%)
    pallas_call x1, Pallas kernels, per_device(): pl.pallas_call(functools.partial(kernel, sizes, capacity), out_shape=(jax...  20.6 us
    unnamed x2, local copies, waits for them, and re-layouts  3.44 us

profile of v2, /device:TPU:0, one launch (start us, length us, event | category | flops | bytes accessed | tf_op | source)
XLA Modules:
  0.0 24.7 jit_solution(195120196509004449)
XLA Ops:
  0.6 20.6 %shard_map.95 = (bf16[2,4,32,256]{3,2,1,0:T(8,128)(2,1)}, f32[4,256,128]{2,1,0:T(8,128)}) custom-call(bf16[4,32,256]{2,1,0:T(8,128)(2,1)} %density.1, bf16[8,27]{1,0:T(8,128)(2,1)} %bitcast.14, f32[8]{0:T(128)} %b1_hbm.1, bf16[16,27]{1,0:T(8,128)(2,1)} %bitcast.13, f32[2]{0:T(128)} %b2_hbm.1, s32[16]{0:T(128)} %bitcast.15, f32[4,256,128]{2,1,0:T(8,128)} %bitcast.10, ...), custom_call_target="tpu_custom_call" | custom-call | tf_op jit(solution)/shard_map/pallas_call | solution.py:389
  21.2 1.6 %copy.12 = bf16[2,4,32,256]{3,2,1,0:T(8,128)(2,1)} copy(bf16[2,4,32,256]{3,2,1,0:T(8,128)(2,1)} %get-tuple-element.8) | data formatting | bytes 262144
  22.8 1.9 %copy.13 = f32[1,1,1,32,2,4,4,128]{7,6,5,4,3,2,1,0:T(4,128)} copy(f32[1,1,1,32,2,4,4,128]{7,6,5,4,3,2,1,0:T(4,128)} %bitcast.11) | data formatting | bytes 1048576

commit v3 on v2

--- a/solution.py
+++ b/solution.py
@@ -134,10 +134,10 @@
 
 def kernel(
     sizes, capacity,
-    density, w1_hbm, b1_hbm, w2_hbm, b2_hbm, owners_hbm, solutes, biomass,
-    fractions, solutes_next,
-    w1_ref, b1_ref, w2_ref, b2_ref, owners_ref, tile, first, second, shifted, hidden, frac, out, arrived, state, state_new, mass_in, mass, gathered,
-    halo_send, halo_recv, brick_send, brick_recv, local_sem, group_sem,
+    density, w1_hbm, b1_hbm, w2_hbm, b2_hbm, owners_hbm,
+    fractions, arrived,
+    w1_ref, b1_ref, w2_ref, b2_ref, owners_ref, tile, first, second, shifted, hidden, frac, out,
+    halo_send, halo_recv, brick_send, brick_recv, local_sem,
 ):
     n, n_gy, n_col = sizes
     slots = n * capacity
@@ -195,8 +195,6 @@
         density, region(tile, (PLACE_Z, PLACE_Y, PLACE_X), (0, 0, 0)), local_sem.at[0]
     )
     own.start()
-    load_state = pltpu.make_async_copy(solutes, state, local_sem.at[1])
-    load_mass = pltpu.make_async_copy(biomass, mass_in, local_sem.at[2])
     pl.semaphore_wait(barrier, expected)
 
     for index, offset in enumerate(AROUND):
@@ -204,9 +202,6 @@
         @pl.when(exists(offset))
         def _():
             halo(offset, index, False).start()
-
-    load_state.start()
-    load_mass.start()
 
     for copy in small:
         copy.wait()
@@ -223,10 +218,6 @@
     keep = jnp.where(
         ((lane == 0) & (here[2] < n_col - 1)) | ((lane == BX - 1) & (here[2] > 0)), 1.0, 0.0
     )
-    load_mass.wait()
-    for g in range(slots // 8):
-        mass[g] = mass_in[g].astype(F32)
-
     own.wait()
     for index, offset in enumerate(AROUND):
 
@@ -294,87 +285,102 @@
             out[d, z] = placed[d * per : (d + 1) * per]
         for j in range(1, n):
             brick_copy(j, z).start()
-    store_frac = pltpu.make_async_copy(frac, fractions, local_sem.at[3])
+    store_frac = pltpu.make_async_copy(frac, fractions, local_sem.at[1])
     store_frac.start()
-
-    load_state.wait()
-
-    def received(j, z):
+    keep_own = pltpu.make_async_copy(out.at[me], arrived.at[me], local_sem.at[2])
+    keep_own.start()
+
+    for j in range(1, n):
         source = lax.rem(me - j + n, n)
-        pltpu.make_async_remote_copy(
-            src_ref=out.at[source, z],
-            dst_ref=arrived.at[source, z],
-            send_sem=brick_send.at[j, z],
-            recv_sem=brick_recv.at[j, z],
-            device_id={"gz": source},
-            device_id_type=MESH,
-        ).wait_recv()
+        for z in range(4):
+            pltpu.make_async_remote_copy(
+                src_ref=out.at[source, z],
+                dst_ref=arrived.at[source, z],
+                send_sem=brick_send.at[j, z],
+                recv_sem=brick_recv.at[j, z],
+                device_id={"gz": source},
+                device_id_type=MESH,
+            ).wait_recv()
+    for index, offset in enumerate(AROUND):
+
+        @pl.when(exists(offset))
+        def _():
+            halo(offset, index, False).wait_send()
+
+    for j in range(1, n):
+        for z in range(4):
+            brick_copy(j, z).wait_send()
+    store_frac.wait()
+    keep_own.wait()
+
+
+def diffusion_kernel(
+    n, capacity,
+    fractions_in, arrived_hbm, solutes, biomass,
+    fractions, solutes_next,
+    arrived, state, state_new, mass_in, mass, gathered,
+    pass_sem, in_sem, out_sem,
+):
+    slots = n * capacity
+    groups = slots // 8
+    per_group = 8 // capacity
+    through = pltpu.make_async_copy(fractions_in, fractions, pass_sem.at[0])
+
+    def loads(g):
+        span = pl.ds(g * per_group, per_group)
+        return [
+            pltpu.make_async_copy(source, target, in_sem.at[g, i])
+            for i, (source, target) in enumerate(
+                (
+                    (arrived_hbm.at[span], arrived.at[span]),
+                    (solutes.at[g], state.at[g]),
+                    (biomass.at[g], mass_in.at[g]),
+                )
+            )
+        ]
+
+    for g in range(groups):
+        for copy in loads(g):
+            copy.start()
+    through.start()
 
     def group_copy(g):
-        return pltpu.make_async_copy(state_new.at[g], solutes_next.at[g], group_sem.at[g])
-
-    def group(g, pore, organic):
+        return pltpu.make_async_copy(state_new.at[g], solutes_next.at[g], out_sem.at[g])
+
+    for g in range(groups):
+        for copy in loads(g):
+            copy.wait()
+        mass[...] = mass_in[g].astype(F32)
+        values = [[None] * 16, [None] * 16]
+        if capacity == 8:
+            for z in range(4):
+                for o in range(2):
+                    for pair in range(2):
+                        at = o * 32 + pair * 16
+                        both = arrived[g, z, at : at + 16, :].astype(F32)
+                        values[o][z * 4 + pair * 2] = both[:8]
+                        values[o][z * 4 + pair * 2 + 1] = both[8:]
+        else:
+            for part in range(per_group):
+                for z in range(4):
+                    block = arrived[g * per_group + part, z].astype(F32)
+                    for row in range(8):
+                        q = row // 4 * 16 + z * 4 + row % 4
+                        gathered[q, part * capacity : (part + 1) * capacity, :] = block[
+                            row * capacity : (row + 1) * capacity
+                        ]
+            values = [[gathered[o * 16 + q] for q in range(16)] for o in range(2)]
         carbon = [state[g, pl.ds(q, 8, stride=32), :] for q in range(16)]
         oxygen = [state[g, pl.ds(16 + q, 8, stride=32), :] for q in range(16)]
-        held = [mass[g, pl.ds(q, 8, stride=16), :] for q in range(16)]
-        carbon, oxygen = diffuse(carbon, oxygen, pore, organic, held, iota((8, BX), 1))
+        held = [mass[pl.ds(q, 8, stride=16), :] for q in range(16)]
+        carbon, oxygen = diffuse(carbon, oxygen, *values, held, iota((8, BX), 1))
         for q in range(16):
             state_new[g, pl.ds(q, 8, stride=32), :] = carbon[q]
             state_new[g, pl.ds(16 + q, 8, stride=32), :] = oxygen[q]
         group_copy(g).start()
-
-    if capacity == 8:
-        for j in range(n):
-            source = lax.rem(me - j + n, n)
-            values = [[None] * 16, [None] * 16]
-            for z in range(4):
-                if j:
-                    received(j, z)
-                ref = arrived if j else out
-                for o in range(2):
-                    for pair in range(2):
-                        at = o * 32 + pair * 16
-                        both = ref[source, z, at : at + 16, :].astype(F32)
-                        values[o][z * 4 + pair * 2] = both[:8]
-                        values[o][z * 4 + pair * 2 + 1] = both[8:]
-            group(source, *values)
-    else:
-        for z in range(4):
-            arrived[me, z] = out[me, z]
-        for j in range(1, n):
-            for z in range(4):
-                received(j, z)
-        for s in range(n):
-            for z in range(4):
-                block = arrived[s, z].astype(F32)
-                for o in range(2):
-                    for y in range(4):
-                        at = (o * 4 + y) * capacity
-                        gathered[o * 16 + z * 4 + y, s * capacity : (s + 1) * capacity, :] = block[
-                            at : at + capacity
-                        ]
-
-        @pl.loop(0, slots // 8)
-        def _(g):
-            start = pl.multiple_of(g * 8, 8)
-            group(
-                g,
-                [gathered[q, pl.ds(start, 8), :] for q in range(16)],
-                [gathered[16 + q, pl.ds(start, 8), :] for q in range(16)],
-            )
-
-    for index, offset in enumerate(AROUND):
-
-        @pl.when(exists(offset))
-        def _():
-            halo(offset, index, False).wait_send()
-
-    for j in range(1, n):
-        for z in range(4):
-            brick_copy(j, z).wait_send()
-    store_frac.wait()
-    for g in range(slots // 8):
+    for g in range(groups):
         group_copy(g).wait()
+    through.wait()
 
 
 def per_device(
@@ -386,13 +392,13 @@
     per = 8 * capacity
     anywhere = pl.BlockSpec(memory_space=pltpu.HBM)
     groups = slots // 8
-    fractions, solutes_next = pl.pallas_call(
+    fractions, arrived = pl.pallas_call(
         functools.partial(kernel, sizes, capacity),
         out_shape=(
             jax.ShapeDtypeStruct((2,) + density.shape, BF16),
-            jax.ShapeDtypeStruct((groups, 256, BX), F32),
+            jax.ShapeDtypeStruct((n, 4, per, BX), BF16),
         ),
-        in_specs=[anywhere] * 8,
+        in_specs=[anywhere] * 6,
         out_specs=(anywhere, anywhere),
         scratch_shapes=[
             pltpu.VMEM((8, 27), BF16),
@@ -407,18 +413,11 @@
             pltpu.VMEM((6, 272, LANES), BF16),
             pltpu.VMEM((2,) + density.shape, BF16),
             pltpu.VMEM((n, 4, per, BX), BF16),
-            pltpu.VMEM((n, 4, per, BX), BF16),
-            pltpu.VMEM((groups, 256, BX), F32),
-            pltpu.VMEM((groups, 256, BX), F32),
-            pltpu.VMEM((groups, 128, BX), BF16),
-            pltpu.VMEM((groups, 128, BX), F32),
-            pltpu.VMEM((32, slots if capacity != 8 else 8, BX), F32),
             pltpu.SemaphoreType.DMA((26,)),
             pltpu.SemaphoreType.DMA((26,)),
             pltpu.SemaphoreType.DMA((n, 4)),
             pltpu.SemaphoreType.DMA((n, 4)),
             pltpu.SemaphoreType.DMA((9,)),
-            pltpu.SemaphoreType.DMA((groups,)),
         ],
         compiler_params=pltpu.CompilerParams(
             collective_id=0, has_side_effects=True, vmem_limit_bytes=64 * 1024 * 1024
@@ -430,6 +429,30 @@
         second_kernel.transpose(1, 2, 0).reshape(16, 27),
         second_bias,
         owners.reshape(-1),
+    )
+    fractions, solutes_next = pl.pallas_call(
+        functools.partial(diffusion_kernel, n, capacity),
+        out_shape=(
+            jax.ShapeDtypeStruct((2,) + density.shape, BF16),
+            jax.ShapeDtypeStruct((groups, 256, BX), F32),
+        ),
+        in_specs=[anywhere] * 4,
+        out_specs=(anywhere, anywhere),
+        scratch_shapes=[
+            pltpu.VMEM((n, 4, per, BX), BF16),
+            pltpu.VMEM((groups, 256, BX), F32),
+            pltpu.VMEM((groups, 256, BX), F32),
+            pltpu.VMEM((groups, 128, BX), BF16),
+            pltpu.VMEM((128, BX), F32),
+            pltpu.VMEM((32, 8, BX), F32),
+            pltpu.SemaphoreType.DMA((1,)),
+            pltpu.SemaphoreType.DMA((groups, 3)),
+            pltpu.SemaphoreType.DMA((groups,)),
+        ],
+        compiler_params=pltpu.CompilerParams(vmem_limit_bytes=64 * 1024 * 1024),
+    )(
+        fractions,
+        arrived,
         solutes.reshape(groups, 256, BX),
         biomass.reshape(groups, 128, BX),
     )

time: 24.9 us -> 25.2 us (1.012)
  Pallas kernels: 20.6 us -> 24.4 us
  local copies, waits for them, and re-layouts: 3.44 us -> 0 us
    pallas_call x0 -> x1, Pallas kernels: none -> 5.24 us  [per_device(): pl.pallas_call(functools.partial(diffusion_kernel, n, capacity), out_shap...]
    unnamed x2 -> x0, local copies, waits for them, and re-layouts: 3.44 us -> none
    pallas_call x1, Pallas kernels: 20.6 us -> 19.1 us  [per_device(): pl.pallas_call(functools.partial(kernel, sizes, capacity), out_shape=(jax...]
where the time goes in v3:
time: 25.2 us; the launch traced here: 25 us
  Pallas kernels  24.4 us (97%)
  between operations  0.64 us (3%)
    pallas_call x1, Pallas kernels, per_device(): pl.pallas_call(functools.partial(kernel, sizes, capacity), out_shape=(jax...  19.1 us
    pallas_call x1, Pallas kernels, per_device(): pl.pallas_call(functools.partial(diffusion_kernel, n, capacity), out_shap...  5.24 us

profile of v3, /device:TPU:0, one launch (start us, length us, event | category | flops | bytes accessed | tf_op | source)
XLA Modules:
  0.0 25.0 jit_solution(2823141271379791752)
XLA Ops:
  0.6 19.1 %shard_map.95 = (bf16[2,4,32,256]{3,2,1,0:T(8,128)(2,1)}, bf16[4,4,64,128]{3,2,1,0:T(8,128)(2,1)}) custom-call(bf16[4,32,256]{2,1,0:T(8,128)(2,1)} %density.1, bf16[8,27]{1,0:T(8,128)(2,1)} %bitcast.13, f32[8]{0:T(128)} %b1_hbm.1, bf16[16,27]{1,0:T(8,128)(2,1)} %bitcast.12, f32[2]{0:T(128)} %b2_hbm.1, s32[16]{0:T(128)} %bitcast.14), custom_call_target="tpu_custom_call" | custom-call | tf_op jit(solution)/shard_map/pallas_call | solution.py:395
  19.8 5.2 %shard_map.96 = (bf16[2,4,32,256]{3,2,1,0:T(8,128)(2,1)}, f32[4,256,128]{2,1,0:T(8,128)}) custom-call(bf16[2,4,32,256]{3,2,1,0:T(8,128)(2,1)} %get-tuple-element.6.fractions_in, bf16[4,4,64,128]{3,2,1,0:T(8,128)(2,1)} %get-tuple-element.7.arrived_hbm, f32[4,256,128]{2,1,0:T(8,128)} %bitcast.10, bf16[4,128,128]{2,1,0:T(8,128)(2,1)} %bitcast.11), custom_call_target="tpu_custom_call" | custom-call | tf_op jit(solution)/shard_map/pallas_call | solution.py:433
